TPU v7x, 128 devices: a whole 4x4x4 slice. The times are simulated.
128 devices in a mesh: blk: 8 (over y, x_lo), grp: 16 (over x_hi, z, core).
Axes of the slice: x: 4 (x_hi: 2, x_lo: 2; x = x_hi * 2 + x_lo), y: 4, z: 4, core: 2. Of those that a mesh axis runs over, the one named last changes fastest.
Arguments:
- record: bfloat16 [16448, 32768], P(None, ('blk', 'grp')), may hold values from -400 to 400
- owner_order: int32 [4, 8], replicated, may hold values from 0 to 15, as said below
Outputs:
- cross_spectra: bfloat16 [4, 2, 16, 32768, 256], P(None, None, None, ('blk', 'grp'))
Inputs may be any that keep to these rules, and one draw needn't show every extreme that they name: `owner_order`: a channel block position within a group.
All inputs are finite; a program needn't handle non-finite values.
Results may differ from a plain program's by a relative error of at most 0.0071.
Values may be sent and summed in bfloat16 or wider, within the bound.
A program may use at most 192 MiB of HBM per device.

v0:
```python
import math

import jax
import jax.numpy as jnp
from jax import lax
from jax.sharding import PartitionSpec as P

WIN = 256
NS = 128
NB = 16
BIN_LO = 8
ROUNDS = 4
HOP = 64


def shifted(value, axis, steps):
    count = lax.axis_size(axis)
    pairs = [(source, (source + steps) % count) for source in range(count)]
    return lax.ppermute(value, axis, pairs)


def broadcast(value, axis, source):
    kept = jnp.where(lax.axis_index(axis) == source, value, 0).astype(value.dtype)
    return lax.psum(kept, axis)


def band_table():
    sample_index = jnp.arange(NS, dtype=jnp.int32)
    bin_index = BIN_LO + jnp.arange(NB, dtype=jnp.int32)
    phase_int = bin_index[:, None] * sample_index[None, :] % NS
    phase = phase_int.astype(jnp.float32) * (2.0 * math.pi / NS)
    taper = 0.5 - 0.5 * jnp.cos(sample_index.astype(jnp.float32) * (2.0 * math.pi / NS))
    scale = 1.0 / math.sqrt(3.0 * NS / 8.0)
    real_rows = taper[None, :] * jnp.cos(phase) * scale
    imag_rows = -taper[None, :] * jnp.sin(phase) * scale
    return jnp.concatenate([real_rows, imag_rows], axis=0).astype(jnp.bfloat16)


def block_spectra(record):
    table = band_table()
    halves = record.reshape(WIN + 1, HOP, record.shape[1])
    first_half = jnp.einsum(
        "kn,hnc->hkc", table[:, :HOP], halves, preferred_element_type=jnp.float32
    )
    second_half = jnp.einsum(
        "kn,hnc->hkc", table[:, HOP:], halves, preferred_element_type=jnp.float32
    )
    wide_halves = halves.astype(jnp.float32)
    half_energy = jnp.sum(wide_halves * wide_halves, axis=1)
    window_rms = jnp.sqrt((half_energy[:-1] + half_energy[1:]) / NS + 1e-05)
    raw = first_half[:-1] + second_half[1:]
    return (raw / window_rms[:, None, :]).astype(jnp.bfloat16)


def cross_stack(own, other):
    real_own, imag_own = (own[:, :NB], own[:, NB:])
    real_other, imag_other = (other[:, :NB], other[:, NB:])
    real_part = jnp.einsum("wfi,wfj->fij", real_own, real_other, preferred_element_type=jnp.float32)
    real_part = real_part + jnp.einsum(
        "wfi,wfj->fij", imag_own, imag_other, preferred_element_type=jnp.float32
    )
    imag_part = jnp.einsum("wfi,wfj->fij", imag_own, real_other, preferred_element_type=jnp.float32)
    imag_part = imag_part - jnp.einsum(
        "wfi,wfj->fij", real_own, imag_other, preferred_element_type=jnp.float32
    )
    return jnp.stack([real_part, imag_part], axis=0) / math.sqrt(WIN)


def body(record, owner_order):
    spectra = block_spectra(record)
    my_group = lax.axis_index("blk")
    results = []
    resident = spectra
    for round_index in range(ROUNDS):
        if round_index > 0:
            resident = shifted(resident, "blk", 1)
        owner_rank = owner_order[round_index, my_group]
        received = broadcast(resident, "grp", owner_rank)
        results.append(cross_stack(spectra, received))
    return jnp.stack(results, axis=0).astype(jnp.bfloat16)


def solution(mesh):
    placed = (P(None, ("blk", "grp")), P())
    return jax.shard_map(
        body,
        mesh=mesh,
        in_specs=placed,
        out_specs=P(None, None, None, ("blk", "grp"), None),
        check_vma=False,
    )
```

profile of v0, /device:TPU:1, one launch (start us, length us, event | category | flops | bytes accessed | tf_op | source)
XLA Modules:
  0.0 586.7 jit_solution(14606508213172173863)
XLA Ops:
  6.6 6.8 %multiply_reduce_fusion = f32[257,256]{1,0:T(8,128)S(1)} fusion(bf16[257,64,256]{2,1,0:T(8,128)(2,1)} %bitcast.49), kind=kLoop, calls=%fused_computation | loop fusion | flops 12566272 | bytes 8684544 | tf_op jit(solution)/shard_map/reduce_sum | solution.py:49
  13.6 4.8 convolution_bitcast_fusion
  18.3 4.6 convolution_bitcast_fusion.1
  23.0 0.7 constant_dynamic-slice_fusion.2
  24.3 8.7 %broadcast_select_fusion.3 = (bf16[256,32,256]{2,1,0:T(8,128)(2,1)}, bf16[256,32,256]{2,1,0:T(8,128)(2,1)S(1)}) fusion(pred[]{:T(512)S(6)} %eq.14, f32[256,256]{1,0:T(8,128)S(1)} %fusion.32, f32[257,32,256]{2,1,0:T(8,128)} %convolution_bitcast_fusion, f32[257,32,256]{2,1,0:T(8,128)} %convolution_bitcast_fusion.1), kind=kLoop, calls=%fused_computation.24 | loop fusion | flops 8388608 | bytes 25427968 | tf_op jit(solution)/shard_map/jit(_where)/select_n | solution.py:23
  33.0 2.0 copy-done.4
  35.0 2.0 collective-permute-start
  37.1 92.6 %collective-permute-done = bf16[256,32,256]{2,1,0:T(8,128)(2,1)S(1)} collective-permute-done((bf16[256,32,256]{2,1,0:T(8,128)(2,1)S(1)}, bf16[256,32,256]{2,1,0:T(8,128)(2,1)S(1)}, u32[]{:S(2)}, u32[]{:S(2)}) %collective-permute-start) | collective-permute-done | bytes 4194336 | tf_op jit(solution)/shard_map/ppermute | solution.py:19
  129.7 2.0 copy-done.8
  131.6 92.9 %collective-permute-done.1 = bf16[256,32,256]{2,1,0:T(8,128)(2,1)} collective-permute-done((bf16[256,32,256]{2,1,0:T(8,128)(2,1)S(1)}, bf16[256,32,256]{2,1,0:T(8,128)(2,1)}, u32[]{:S(2)}, u32[]{:S(2)}) %collective-permute-start.1) | collective-permute-done | bytes 4194336 | tf_op jit(solution)/shard_map/ppermute | solution.py:19
  226.5 2.3 broadcast_select_fusion.2
  228.8 2.2 broadcast_select_fusion.1
  231.0 85.8 %collective-permute-done.2 = bf16[256,32,256]{2,1,0:T(8,128)(2,1)} collective-permute-done((bf16[256,32,256]{2,1,0:T(8,128)(2,1)}, bf16[256,32,256]{2,1,0:T(8,128)(2,1)}, u32[]{:S(2)}, u32[]{:S(2)}) %collective-permute-start.2) | collective-permute-done | bytes 4194336 | tf_op jit(solution)/shard_map/ppermute | solution.py:19
  316.8 2.2 broadcast_select_fusion
  319.0 4.6 fusion.54
  323.6 3.0 copy.5
  326.6 4.3 copy.3
  330.9 190.9 %all-reduce.3.cloned.1.call-done = (bf16[256,32,256]{2,1,0:T(8,128)(2,1)}, bf16[256,32,256]{2,1,0:T(8,128)(2,1)}, bf16[256,32,256]{2,1,0:T(8,128)(2,1)}, bf16[256,32,256]{2,1,0:T(8,128)(2,1)}) async-done(((bf16[256,32,256]{2,1,0:T(8,128)(2,1)}, bf16[256,32,256]{2,1,0:T(8,128)(2,1)}, bf16[256,32,256]{2,1,0:T(8,128)(2,1)}, bf16[256,32,256]{2,1,0:T(8,128)(2,1)}), (bf16[256,32,256]{2,1,0:T(8,128)(2,1)}, ...) | async-done | bytes 16777232 | tf_op jit(solution)/shard_map/psum | solution.py:24
  521.8 2.7 fusion.53
  524.7 1.0 fusion.6
  525.7 1.0 fusion.8
  526.7 1.2 copy-done.7
  527.9 0.3 fusion.52
  528.2 3.0 fusion.12
  531.2 1.0 fusion.14
  532.2 1.2 copy-done.6
  533.4 0.3 fusion.51
  533.7 3.0 fusion.18
  536.7 1.0 fusion.20
  537.7 2.5 fusion.50
  540.2 2.9 fusion.26
  543.2 2.9 fusion.28
  546.1 1.1 subtract_bitcast_fusion
  547.2 1.0 add_bitcast_fusion
  548.2 1.1 copy-done.3
  549.4 1.2 subtract_bitcast_fusion.1
  550.5 1.3 add_bitcast_fusion.1
  551.8 3.4 subtract_bitcast_fusion.2
  555.1 1.0 add_bitcast_fusion.2
  556.2 3.4 subtract_bitcast_fusion.3
  559.6 5.3 add_bitcast_fusion.3
  564.9 2.5 fusion.5
  567.4 1.0 fusion.4
  568.5 1.1 fusion.3
  569.6 1.1 copy-done.2
  570.6 1.0 fusion.2
  571.7 1.1 copy-done.5
  572.8 7.0 %pad_maximum_fusion = bf16[4,2,16,256,256]{4,3,2,1,0:T(8,128)(2,1)} fusion(bf16[1,2,16,256,256]{4,3,2,1,0:T(8,128)(2,1)S(1)} %copy-done.5, bf16[1,2,16,256,256]{4,3,2,1,0:T(8,128)(2,1)S(1)} %fusion.4, bf16[1,2,16,256,256]{4,3,2,1,0:T(8,128)(2,1)S(1)} %fusion.3, bf16[1,2,16,256,256]{4,3,2,1,0:T(8,128)(2,1)S(1)} %fusion.2), kind=kLoop, calls=%fused_computation.1 | loop fusion | flops 25165824 | bytes 33554432 | tf_op jit(solution)/shard_map/stack | solution.py:80
  (21 shorter events, 0.5 us)
Async XLA Ops:
  6.5 515.3 %all-reduce.3.cloned.1.call-start = ((), (), s32[]{:S(2)}) async-start(), calls=%async_computation | async-start | bytes 33554432 | tf_op jit(solution)/shard_map/psum | solution.py:24
  6.6 7.0 %copy-start.1 = (bf16[16448,256]{1,0:T(8,128)(2,1)S(1)}, bf16[16448,256]{1,0:T(8,128)(2,1)}, u32[]{:S(2)}) copy-start(bf16[16448,256]{1,0:T(8,128)(2,1)} %param.2) | copy-start | bytes 25264132
  18.3 4.7 copy-start.9
  33.0 2.0 copy-start.4
  35.0 94.7 %collective-permute-start = (bf16[256,32,256]{2,1,0:T(8,128)(2,1)S(1)}, bf16[256,32,256]{2,1,0:T(8,128)(2,1)S(1)}, u32[]{:S(2)}, u32[]{:S(2)}) collective-permute-start(bf16[256,32,256]{2,1,0:T(8,128)(2,1)S(1)} %get-tuple-element.10), channel_id=1, source_target_pairs={{0,16},{16,32},{32,48},{48,64},{64,80},{80,96},{96,112},{112,0},{1... | collective-permute-start | bytes 12582920 | tf_op jit(solution)/shard_map/ppermute | solution.py:19
  129.7 2.0 copy-start.8
  131.6 92.9 %collective-permute-start.1 = (bf16[256,32,256]{2,1,0:T(8,128)(2,1)S(1)}, bf16[256,32,256]{2,1,0:T(8,128)(2,1)}, u32[]{:S(2)}, u32[]{:S(2)}) collective-permute-start(bf16[256,32,256]{2,1,0:T(8,128)(2,1)S(1)} %collective-permute-done), channel_id=1, source_target_pairs={{0,16},{16,32},{32,48},{48,64},{64,80},{80,96},{96,112},{112,0},{1... | collective-permute-start | bytes 12582920 | tf_op jit(solution)/shard_map/ppermute | solution.py:19
  224.6 92.2 %collective-permute-start.2 = (bf16[256,32,256]{2,1,0:T(8,128)(2,1)}, bf16[256,32,256]{2,1,0:T(8,128)(2,1)}, u32[]{:S(2)}, u32[]{:S(2)}) collective-permute-start(bf16[256,32,256]{2,1,0:T(8,128)(2,1)} %collective-permute-done.1), channel_id=1, source_target_pairs={{0,16},{16,32},{32,48},{48,64},{64,80},{80,96},{96,112},{112,0},{1... | collective-permute-start | bytes 12582920 | tf_op jit(solution)/shard_map/ppermute | solution.py:19
  521.8 2.9 copy-start
  525.7 2.2 copy-start.7
  531.2 2.2 copy-start.6
  547.2 2.2 copy-start.3
  568.5 2.2 copy-start.2
  570.6 2.2 copy-start.5
Sparse Core Ops, SparseCore 0:
  319.1 202.6 all-reduce.2
where the time goes:
time: 589 us; the launch traced here: 587 us
  waiting for transfers between devices  462 us (78%)
  matrix products  42.6 us (7%)
  other arithmetic  35.2 us (6%)
  local copies, waits for them, and re-layouts  28.4 us (5%)
  between operations  16.1 us (3%)
    ppermute x3, waiting for transfers between devices, shifted(): return lax.ppermute(value, axis, pairs)  271 us
    psum x1, waiting for transfers between devices, broadcast(): return lax.psum(kept, axis)  191 us
    select_n x4, other arithmetic, broadcast(): jnp.where(lax.axis_index(axis) == source, value, 0).astype(value.dtype)  15.4 us
    slice x3, local copies, waits for them, and re-layouts, cross_stack(): real_own, imag_own = (own[:, :NB], own[:, NB:])  11.9 us
  transfers between devices with their start and end apart: 4, of which 4 were waited for; matrix products, arithmetic and copies ran while one was open for 3% of the time, Pallas kernels for 0%

commit v1 on v0

v1 whole, which is shorter than its diff:
```python
import functools
import math

import jax
import jax.numpy as jnp
import numpy as np
from jax import lax
from jax.experimental import pallas as pl
from jax.experimental.pallas import tpu as pltpu
from jax.sharding import PartitionSpec as P

WIN = 256
NS = 128
NB = 16
BIN_LO = 8
ROUNDS = 4
HOP = 64
CH = 256
GW = 8
STEPW = 32
NCH = 2
PIECE = 1024
ROWS = PIECE // NCH
MESH = pl.DeviceIdType.MESH


def band_table():
    sample_index = np.arange(NS, dtype=np.int64)
    bin_index = BIN_LO + np.arange(NB, dtype=np.int64)
    phase = (bin_index[:, None] * sample_index[None, :] % NS) * (2.0 * math.pi / NS)
    taper = 0.5 - 0.5 * np.cos(sample_index * (2.0 * math.pi / NS))
    scale = 1.0 / math.sqrt(3.0 * NS / 8.0)
    real_rows = taper[None, :] * np.cos(phase) * scale
    imag_rows = -taper[None, :] * np.sin(phase) * scale
    return np.stack([real_rows, imag_rows], axis=1).reshape(2 * NB, NS)


def banded_table():
    table = band_table()
    wide = np.zeros((2 * NB, GW, HOP * (GW + 1)), np.float32)
    for w in range(GW):
        wide[:, w, w * HOP : w * HOP + NS] = table
    return wide.reshape(2 * NB * GW, HOP * (GW + 1)).astype(jnp.bfloat16)


def spectra_kernel(t_ref, main_ref, tail_ref, o_ref):
    parts = []
    for s in range(STEPW // GW):
        lo = s * GW * HOP
        if s < STEPW // GW - 1:
            x = main_ref[lo : lo + (GW + 1) * HOP, :]
        else:
            x = jnp.concatenate([main_ref[lo : lo + GW * HOP, :], tail_ref[...]], axis=0)
        raw = jnp.dot(t_ref[...], x, preferred_element_type=jnp.float32)
        wide = x.astype(jnp.float32)
        energy = jnp.sum((wide * wide).reshape(GW + 1, HOP, CH), axis=1)
        inv = 1.0 / jnp.sqrt((energy[:GW] + energy[1:]) / NS + 1e-05)
        parts.append(raw.reshape(2 * NB, GW, CH) * inv[None])
        if s % 2 == 1:
            both = jnp.concatenate(parts, axis=1).astype(jnp.bfloat16)
            o_ref[:, (s - 1) * GW : (s + 1) * GW, :] = both
            parts = []


def spectra(record):
    steps = WIN // STEPW
    return pl.pallas_call(
        spectra_kernel,
        grid=(steps,),
        out_shape=jax.ShapeDtypeStruct((2 * NB, WIN, CH), jnp.bfloat16),
        in_specs=[
            pl.BlockSpec((2 * NB * GW, HOP * (GW + 1)), lambda g: (0, 0)),
            pl.BlockSpec((STEPW * HOP, CH), lambda g: (g, 0)),
            pl.BlockSpec((HOP, CH), lambda g: ((g + 1) * STEPW, 0)),
        ],
        out_specs=pl.BlockSpec((2 * NB, STEPW, CH), lambda g: (0, g, 0)),
        compiler_params=pltpu.CompilerParams(vmem_limit_bytes=48 * 2**20),
        name="spectra",
    )(jnp.asarray(banded_table()), record, record)


NSEM = 48


def exchange_kernel(order_ref, s_ref, g_ref, *scratch):
    it = iter(scratch)
    a_buf = [next(it) for _ in range(NCH)]
    b_send = [[next(it) for _ in range(2)] for _ in range(NCH)]
    b_recv = [[next(it) for _ in range(ROUNDS)] for _ in range(NCH)]
    merged = [[next(it) for _ in range(ROUNDS)] for _ in range(NCH)]
    final = [[next(it) for _ in range(ROUNDS)] for _ in range(NCH)]
    hop1 = [next(it) for _ in range(NCH)]
    ssem, rsem, lsem = next(it), next(it), next(it)

    blk = lax.axis_index("blk")
    grp = lax.axis_index("grp")
    y, par = blk // 2, blk % 2
    xhi, z, core = grp // 8, (grp // 2) % 4, grp % 2

    def chip(dx, dy, dz, other):
        x = (xhi * 2 + par + dx + 4) % 4
        yy = (y + dy + 4) % 4
        zz = (z + dz + 4) % 4
        c = 1 - core if other else core
        return (yy * 2 + x % 2, (x // 2) * 8 + zz * 2 + c)

    def rows(j):
        return pl.ds(j * ROWS, ROWS)

    counters = [[0] for _ in range(NCH)]

    def remote(j, src, dst, device):
        k = counters[j][0]
        counters[j][0] += 1
        cp = pltpu.make_async_remote_copy(
            src_ref=src, dst_ref=dst, send_sem=ssem.at[j, k], recv_sem=rsem.at[j, k],
            device_id=device, device_id_type=MESH,
        )
        cp.start()
        return cp

    def copy_rows(dst, load):
        step = 64

        def run(i, carry):
            at = pl.ds(i * step, step)
            dst[at, :] = load(at)
            return carry

        lax.fori_loop(0, ROWS // step, run, 0)

    sent = []

    a_copies = [[] for _ in range(NCH)]
    slot = z * 2 + core

    def start_a(j):
        for dz, other in ((2, 0), (2, 1), (1, 0), (3, 0), (1, 1), (3, 1), (0, 1)):
            zz = (z + dz) % 4
            c = 1 - core if other else core
            a_copies[j].append(
                remote(j, s_ref.at[zz * 2 + c, rows(j)], a_buf[j].at[slot], chip(0, 0, dz, other))
            )
        own = pltpu.make_async_copy(s_ref.at[slot, rows(j)], a_buf[j].at[slot], lsem.at[j, 0])
        own.start()
        return own

    owns = {}
    b_copies = [[[] for _ in range(ROUNDS)] for _ in range(NCH)]
    h_copies = [[None] * ROUNDS for _ in range(NCH)]
    c_copies = [[None] * ROUNDS for _ in range(NCH)]
    locals_ = []

    def pick_and_send(j):
        owns[j].wait()
        for cp in a_copies[j]:
            cp.wait_recv()
        for r in range(ROUNDS):
            owner = order_ref[r, (blk + r) % 8] % 8
            if r % 2 == 0:
                dst = b_recv[j][r].at[xhi]
            else:
                dst = b_send[j][r // 2]
            copy_rows(dst, lambda at: a_buf[j][owner, at, :])
            for dx in ((2,) if r % 2 == 0 else (1, -1)):
                b_copies[j][r].append(remote(j, dst, b_recv[j][r].at[xhi], chip(dx, 0, 0, 0)))

    def merge_and_hop(j):
        for r in range(ROUNDS):
            for cp in b_copies[j][r]:
                cp.wait_recv()
            source = blk if r % 2 == 0 else blk + 1 - 2 * par
            column = order_ref[r, (source + r) % 8] // 8
            dst = final[j][r] if r == 0 else merged[j][r]
            copy_rows(dst, lambda at: b_recv[j][r][column, at, :])
            if r == 0:
                gather(j, r)
            else:
                dy = 2 - par if r == 3 else 1
                land = hop1[j] if r == 1 else final[j][r]
                h_copies[j][r] = remote(j, dst, land, chip(0, dy, 0, 0))

    def hopped(j):
        for r in range(1, ROUNDS):
            h_copies[j][r].wait_recv()
            if r == 1:
                copy_rows(
                    final[j][r],
                    lambda at: jnp.where(par == 0, hop1[j][at, :], merged[j][r][at, :]),
                )
            gather(j, r)

    def place(r, zz, c, j):
        return g_ref.at[r, zz * 2 + c, rows(j)]

    def half(r, zz, c, j, h):
        return g_ref.at[r, zz * 2 + c, pl.ds(j * ROWS + h * (ROWS // 2), ROWS // 2)]

    def gather(j, r):
        up = remote(j, final[j][r], place(r, z, core, j), chip(0, 0, 1, 0))
        down = remote(j, final[j][r], place(r, z, core, j), chip(0, 0, -1, 0))
        side = remote(j, final[j][r], place(r, z, core, j), chip(0, 0, 0, 1))
        own = pltpu.make_async_copy(final[j][r], place(r, z, core, j), lsem.at[j, 1 + r])
        own.start()
        locals_.append(own)
        c_copies[j][r] = [up, down, side]

    def forward(j, r):
        up, down, side = c_copies[j][r]
        below, above = (z + 3) % 4, (z + 1) % 4
        up.wait_recv()
        f_up = remote(j, half(r, below, core, j, 0), half(r, below, core, j, 0), chip(0, 0, 1, 0))
        s_below = remote(j, place(r, below, core, j), place(r, below, core, j), chip(0, 0, 0, 1))
        down.wait_recv()
        f_down = remote(j, half(r, above, core, j, 1), half(r, above, core, j, 1), chip(0, 0, -1, 0))
        s_above = remote(j, place(r, above, core, j), place(r, above, core, j), chip(0, 0, 0, 1))
        c_copies[j][r] += [f_up, f_down, s_below, s_above]

    def finish(j, r):
        up, down, side, f_up, f_down, s_below, s_above = c_copies[j][r]
        f_up.wait_recv()
        f_down.wait_recv()
        far = (z + 2) % 4
        s_far = remote(j, place(r, far, core, j), place(r, far, core, j), chip(0, 0, 0, 1))
        for cp in (side, s_below, s_above, s_far):
            sent.append(cp)
        c_copies[j][r].append(s_far)

    owns[0] = start_a(0)
    if NCH > 1:
        owns[1] = start_a(1)
    stages = NCH + 4
    for t in range(stages):
        if t < NCH:
            pick_and_send(t)
            if t + 2 < NCH:
                owns[t + 2] = start_a(t + 2)
        if 0 <= t - 1 < NCH:
            merge_and_hop(t - 1)
        if 0 <= t - 2 < NCH:
            forward(t - 2, 0)
            hopped(t - 2)
        if 0 <= t - 3 < NCH:
            for r in range(1, ROUNDS):
                forward(t - 3, r)
            finish(t - 3, 0)
        if 0 <= t - 4 < NCH:
            for r in range(1, ROUNDS):
                finish(t - 4, r)
    for cp in sent:
        cp.wait_recv()
    for cp in locals_:
        cp.wait()
    for j in range(NCH):
        for cp in a_copies[j]:
            cp.wait_send()
        for r in range(ROUNDS):
            for cp in b_copies[j][r]:
                cp.wait_send()
            if h_copies[j][r] is not None:
                h_copies[j][r].wait_send()
            for cp in c_copies[j][r]:
                cp.wait_send()


def exchange(order, s):
    bf16 = jnp.bfloat16
    buf = lambda *lead: pltpu.VMEM(lead + (ROWS, CH), bf16)
    scratch = [buf(8) for _ in range(NCH)]
    scratch += [buf() for _ in range(2 * NCH)]
    scratch += [buf(2) for _ in range(ROUNDS * NCH)]
    scratch += [buf() for _ in range(ROUNDS * NCH)]
    scratch += [buf() for _ in range(ROUNDS * NCH)]
    scratch += [buf() for _ in range(NCH)]
    scratch += [
        pltpu.SemaphoreType.DMA((NCH, NSEM)),
        pltpu.SemaphoreType.DMA((NCH, NSEM)),
        pltpu.SemaphoreType.DMA((NCH, 1 + ROUNDS)),
    ]
    return pl.pallas_call(
        exchange_kernel,
        out_shape=jax.ShapeDtypeStruct((ROUNDS, 8, PIECE, CH), bf16),
        in_specs=[
            pl.BlockSpec(memory_space=pltpu.SMEM),
            pl.BlockSpec(memory_space=pl.ANY),
        ],
        out_specs=pl.BlockSpec(memory_space=pl.ANY),
        scratch_shapes=scratch,
        compiler_params=pltpu.CompilerParams(
            has_side_effects=True, vmem_limit_bytes=56 * 2**20
        ),
        name="exchange",
    )(order, s.reshape(8, PIECE, CH))


def cross_kernel(own_ref, other_ref, o_ref):
    x = own_ref[0]
    p, q = x[:WIN].astype(jnp.float32), x[WIN:].astype(jnp.float32)
    scale = 1.0 / math.sqrt(WIN)
    pt = (p.T * scale).astype(jnp.bfloat16)
    qt = (q.T * scale).astype(jnp.bfloat16)
    left = jnp.concatenate(
        [jnp.concatenate([pt, qt], axis=1), jnp.concatenate([qt, -pt], axis=1)], axis=0
    )
    for r in range(ROUNDS):
        out = jnp.dot(left, other_ref[r, 0], preferred_element_type=jnp.float32)
        o_ref[r, 0, 0] = out[:CH].astype(jnp.bfloat16)
        o_ref[r, 1, 0] = out[CH:].astype(jnp.bfloat16)


def cross(s, g):
    return pl.pallas_call(
        cross_kernel,
        grid=(NB,),
        out_shape=jax.ShapeDtypeStruct((ROUNDS, 2, NB, CH, CH), jnp.bfloat16),
        in_specs=[
            pl.BlockSpec((1, 2 * WIN, CH), lambda f: (f, 0, 0)),
            pl.BlockSpec((ROUNDS, 1, 2 * WIN, CH), lambda f: (0, f, 0, 0)),
        ],
        out_specs=pl.BlockSpec((ROUNDS, 2, 1, CH, CH), lambda f: (0, 0, f, 0, 0)),
        compiler_params=pltpu.CompilerParams(vmem_limit_bytes=48 * 2**20),
        name="cross",
    )(s.reshape(NB, 2 * WIN, CH), g.reshape(ROUNDS, NB, 2 * WIN, CH))


def body(record, owner_order):
    s = spectra(record)
    g = exchange(owner_order, s)
    return cross(s, g)


def solution(mesh):
    placed = (P(None, ("blk", "grp")), P())
    return jax.shard_map(
        body,
        mesh=mesh,
        in_specs=placed,
        out_specs=P(None, None, None, ("blk", "grp"), None),
        check_vma=False,
    )
```

time: 589 us -> 182 us (0.31)
  waiting for transfers between devices: 462 us -> 0 us
  Pallas kernels: 0 us -> 178 us
  matrix products: 42.6 us -> 0 us
  other arithmetic: 35.2 us -> 0 us
  local copies, waits for them, and re-layouts: 28.4 us -> 2.98 us
  between operations: 16.1 us -> 0.03 us
    ppermute x3 -> x0, waiting for transfers between devices: 271 us -> none  [shifted(): return lax.ppermute(value, axis, pairs)]
    psum x1 -> x0, waiting for transfers between devices: 191 us -> none  [broadcast(): return lax.psum(kept, axis)]
    pallas_call x0 -> x3, Pallas kernels: none -> 178 us  [the longest x1 149 us: exchange(): pl.pallas_call(exchange_kernel, out_shape=jax.ShapeDtypeStruct((ROUNDS, 8...]
    dot_general x18 -> x0, matrix products: 42.6 us -> none  [the longest x4 10.3 us: cross_stack(): jnp.einsum('wfi,wfj->fij', real_own, imag_other, preferred_element_type=j...]
    slice x7 -> x0, local copies, waits for them, and re-layouts: 17.8 us -> none  [the longest x3 11.9 us: cross_stack(): real_own, imag_own = (own[:, :NB], own[:, NB:])]
    select_n x4 -> x0, other arithmetic: 15.4 us -> none  [broadcast(): jnp.where(lax.axis_index(axis) == source, value, 0).astype(value.dtype)]
    another operation x6 -> x0, other arithmetic: 12.8 us -> none  [the longest x1 7.01 us: body(): return jnp.stack(results, axis=0).astype(jnp.bfloat16)]
    unnamed x20 -> x6, local copies, waits for them, and re-layouts: 9.96 us -> 2.98 us
  transfers between devices with their start and end apart: 4 -> 0, of which waited for: 4 -> 0; matrix products, arithmetic and copies ran while one was open for 3% -> 0% of each run, Pallas kernels for 0% -> 0%
where the time goes in v1:
time: 182 us
  Pallas kernels  178 us (98%)
  local copies, waits for them, and re-layouts  2.98 us (2%)
    pallas_call x1, Pallas kernels, exchange(): pl.pallas_call(exchange_kernel, out_shape=jax.ShapeDtypeStruct((ROUNDS, 8...  149 us
    pallas_call x1, Pallas kernels, cross(): pl.pallas_call(cross_kernel, grid=(NB,), out_shape=jax.ShapeDtypeStruct((...  21 us
    pallas_call x1, Pallas kernels, spectra(): pl.pallas_call(spectra_kernel, grid=(steps,), out_shape=jax.ShapeDtypeStr...  8.29 us

profile of v1, /device:TPU:1, one launch (start us, length us, event | category | flops | bytes accessed | tf_op | source)
XLA Modules:
  0.0 181.5 jit_solution(229203145760623268)
XLA Ops:
  0.0 0.0 copy-start.2
  0.0 1.0 copy-done.2
  1.0 8.3 %spectra.1 = bf16[32,256,256]{2,1,0:T(8,128)(2,1)S(1)} custom-call(bf16[256,576]{1,0:T(8,128)(2,1)S(1)} %copy-done.2, bf16[16448,256]{1,0:T(8,128)(2,1)} %tail_ref.1, bf16[16448,256]{1,0:T(8,128)(2,1)} %tail_ref.1), custom_call_target="tpu_custom_call" | custom-call | tf_op jit(solution)/shard_map/spectra/pallas_call | solution.py:67
  9.3 0.0 copy-start
  9.3 2.0 %copy-done = bf16[32,256,256]{2,1,0:T(8,128)(2,1)} copy-done((bf16[32,256,256]{2,1,0:T(8,128)(2,1)}, bf16[32,256,256]{2,1,0:T(8,128)(2,1)S(1)}, u32[]{:S(2)}) %copy-start) | copy-done | bytes 4194328
  11.3 0.0 copy-start.1
  11.3 149.2 %exchange.1 = bf16[4,8,1024,256]{3,2,1,0:T(8,128)(2,1)} custom-call(s32[4,8]{1,0:T(4,128)} %order_ref.1, bf16[8,1024,256]{2,1,0:T(8,128)(2,1)} %bitcast.3), custom_call_target="tpu_custom_call" | custom-call | tf_op jit(solution)/shard_map/exchange/pallas_call | solution.py:280
  160.5 0.0 copy-done.1
  160.5 21.0 %cross.1 = bf16[4,2,16,256,256]{4,3,2,1,0:T(8,128)(2,1)} custom-call(bf16[16,512,256]{2,1,0:T(8,128)(2,1)S(1)} %bitcast.4, bf16[4,16,512,256]{3,2,1,0:T(8,128)(2,1)} %bitcast.5), custom_call_target="tpu_custom_call" | custom-call | tf_op jit(solution)/shard_map/cross/pallas_call | solution.py:312
Async XLA Ops:
  0.0 1.0 copy-start.2
  9.3 2.0 %copy-start = (bf16[32,256,256]{2,1,0:T(8,128)(2,1)}, bf16[32,256,256]{2,1,0:T(8,128)(2,1)S(1)}, u32[]{:S(2)}) copy-start(bf16[32,256,256]{2,1,0:T(8,128)(2,1)S(1)} %spectra.1) | copy-start | bytes 12582916
  11.3 149.2 %copy-start.1 = (bf16[32,256,256]{2,1,0:T(8,128)(2,1)S(1)}, bf16[32,256,256]{2,1,0:T(8,128)(2,1)}, u32[]{:S(2)}) copy-start(bf16[32,256,256]{2,1,0:T(8,128)(2,1)} %copy-done) | copy-start | bytes 12582916

commit v2 on v1

v2 whole, which is shorter than its diff:
```python
import functools
import math

import jax
import jax.numpy as jnp
import numpy as np
from jax import lax
from jax.experimental import pallas as pl
from jax.experimental.pallas import tpu as pltpu
from jax.sharding import PartitionSpec as P

WIN = 256
NS = 128
NB = 16
BIN_LO = 8
ROUNDS = 4
HOP = 64
CH = 256
GW = 8
STEPW = 16
PIECE = 1024
PLAN = ((2, True), (2, False)) * 4
AHEAD = 2
AGES = (0, 2, 4, 6, 8)
MESH = pl.DeviceIdType.MESH


def band_table():
    sample_index = np.arange(NS, dtype=np.int64)
    bin_index = BIN_LO + np.arange(NB, dtype=np.int64)
    phase = (bin_index[:, None] * sample_index[None, :] % NS) * (2.0 * math.pi / NS)
    taper = 0.5 - 0.5 * np.cos(sample_index * (2.0 * math.pi / NS))
    scale = 1.0 / math.sqrt(3.0 * NS / 8.0)
    real_rows = taper[None, :] * np.cos(phase) * scale
    imag_rows = -taper[None, :] * np.sin(phase) * scale
    return np.stack([real_rows, imag_rows], axis=1).reshape(2 * NB, NS)


def banded_table():
    table = band_table()
    wide = np.zeros((2 * NB, GW, HOP * (GW + 1)), np.float32)
    for w in range(GW):
        wide[:, w, w * HOP : w * HOP + NS] = table
    return wide.reshape(2 * NB * GW, HOP * (GW + 1)).astype(jnp.bfloat16)


def spectra_kernel(t_ref, main_ref, tail_ref, o_ref):
    parts = []
    for s in range(STEPW // GW):
        lo = s * GW * HOP
        if s < STEPW // GW - 1:
            x = main_ref[lo : lo + (GW + 1) * HOP, :]
        else:
            x = jnp.concatenate([main_ref[lo : lo + GW * HOP, :], tail_ref[...]], axis=0)
        raw = jnp.dot(t_ref[...], x, preferred_element_type=jnp.float32)
        wide = x.astype(jnp.float32)
        energy = jnp.sum((wide * wide).reshape(GW + 1, HOP, CH), axis=1)
        inv = 1.0 / jnp.sqrt((energy[:GW] + energy[1:]) / NS + 1e-05)
        parts.append(raw.reshape(2 * NB, GW, CH) * inv[None])
        if s % 2 == 1:
            both = jnp.concatenate(parts, axis=1).astype(jnp.bfloat16)
            o_ref[:, 0, :, (s - 1) * GW : (s + 1) * GW, :] = both.reshape(8, 4, 2 * GW, CH)
            parts = []


def spectra(record):
    steps = WIN // STEPW
    out = pl.pallas_call(
        spectra_kernel,
        grid=(steps,),
        out_shape=jax.ShapeDtypeStruct((8, steps, 4, STEPW, CH), jnp.bfloat16),
        in_specs=[
            pl.BlockSpec((2 * NB * GW, HOP * (GW + 1)), lambda g: (0, 0)),
            pl.BlockSpec((STEPW * HOP, CH), lambda g: (g, 0)),
            pl.BlockSpec((HOP, CH), lambda g: ((g + 1) * STEPW, 0)),
        ],
        out_specs=pl.BlockSpec((8, 1, 4, STEPW, CH), lambda g: (0, g, 0, 0, 0)),
        compiler_params=pltpu.CompilerParams(vmem_limit_bytes=48 * 2**20),
        name="spectra",
    )(jnp.asarray(banded_table()), record, record)
    return out.reshape(8, PIECE, CH)


NSEM = 32
WB_ROWS = 4 * STEPW
CHUNKS = []
for blocks, shared in PLAN:
    first = CHUNKS[-1][0] + CHUNKS[-1][1] if CHUNKS else 0
    CHUNKS.append((first, blocks * WB_ROWS, shared))
NCH = len(CHUNKS)


def exchange_kernel(order_ref, s_ref, g_ref, *scratch):
    it = iter(scratch)
    a_buf = [next(it) for _ in range(NCH)]
    b_send = [next(it) for _ in range(NCH)]
    b_recv = [next(it) for _ in range(NCH)]
    final = [next(it) for _ in range(NCH)]
    ssem, rsem, lsem = next(it), next(it), next(it)

    blk = lax.axis_index("blk")
    grp = lax.axis_index("grp")
    y, par = blk // 2, blk % 2
    xhi, z, core = grp // 8, (grp // 2) % 4, grp % 2
    slot = z * 2 + core
    below, above, far = (z + 3) % 4, (z + 1) % 4, (z + 2) % 4

    def device(dx, dy, dz, other):
        x = (xhi * 2 + par + dx + 4) % 4
        yy = (y + dy + 4) % 4
        zz = (z + dz + 4) % 4
        c = 1 - core if other else core
        return (yy * 2 + x % 2, (x // 2) * 8 + zz * 2 + c)

    counters = [0] * NCH
    everything = []

    def remote(j, src, dst, target):
        k = counters[j]
        counters[j] += 1
        cp = pltpu.make_async_remote_copy(
            src_ref=src, dst_ref=dst, send_sem=ssem.at[j, k], recv_sem=rsem.at[j, k],
            device_id=target, device_id_type=MESH,
        )
        cp.start()
        everything.append(cp)
        return cp

    def copy_rows(count, store, load):
        step = 32

        def run(i, carry):
            at = pl.multiple_of(i * step, step)
            store(at, step, load(at, step))
            return carry

        lax.fori_loop(0, count // step, run, 0)

    def width(j):
        return CHUNKS[j][1] // 2

    def place(zz, j, column, part=None):
        w = width(j)
        lo = CHUNKS[j][0] + column * w
        if part is not None and CHUNKS[j][2]:
            w = w // 2
            lo = lo + part * w
        elif part is not None:
            lo = CHUNKS[j][0] + part * w
        return g_ref.at[:, zz * 2 + core, pl.ds(pl.multiple_of(lo, 16), w)]

    def gathered(zz, j):
        if CHUNKS[j][2]:
            return place(zz, j, xhi)
        return g_ref.at[:, zz * 2 + core, pl.ds(CHUNKS[j][0], CHUNKS[j][1])]

    a_copies = [[] for _ in range(NCH)]
    locals_ = [[] for _ in range(NCH)]

    def start_a(j):
        rows = pl.ds(CHUNKS[j][0], CHUNKS[j][1])
        for dz, other in ((2, 0), (2, 1), (1, 0), (3, 0), (1, 1), (3, 1), (0, 1)):
            zz = (z + dz) % 4
            c = 1 - core if other else core
            a_copies[j].append(
                remote(j, s_ref.at[zz * 2 + c, rows], a_buf[j].at[slot], device(0, 0, dz, other))
            )
        own = pltpu.make_async_copy(s_ref.at[slot, rows], a_buf[j].at[slot], lsem.at[j, 0])
        own.start()
        locals_[j].append(own)

    b_copies = [[] for _ in range(NCH)]

    def pick_and_send(j):
        locals_[j][0].wait()
        for cp in a_copies[j]:
            cp.wait_recv()
        w = width(j)
        for r in range(ROUNDS):
            owner = order_ref[r, (blk + r) % 8] % 8

            if r == 0:
                base = pl.multiple_of(xhi * w, 16)

                def keep(at, n, value):
                    b_recv[j][0, xhi, pl.ds(at, n), :] = value

                copy_rows(w, keep, lambda at, n: a_buf[j][owner, pl.ds(base + at, n), :])

            def store(at, n, value):
                b_send[j][r, pl.ds(at, n), :] = value

            copy_rows(CHUNKS[j][1], store, lambda at, n: a_buf[j][owner, pl.ds(at, n), :])
            moves = (
                ((2, 0),),
                ((1, par), (-1, par)),
                ((0, 1), (2, 1)),
                ((1, 1 + par), (-1, 1 + par)),
            )[r]
            for dx, dy in moves:
                column = ((xhi * 2 + par + dx + 4) % 4) // 2
                src = b_send[j].at[r, pl.ds(pl.multiple_of(column * w, 16), w)]
                b_copies[j].append(
                    remote(j, src, b_recv[j].at[r, xhi], device(dx, dy, 0, 0))
                )

    c_copies = [None] * NCH
    x_copies = [[] for _ in range(NCH)]
    sides = []

    def spread(j, zz, src):
        sides.append(remote(j, src, gathered(zz, j), device(0, 0, 0, 1)))
        if CHUNKS[j][2]:
            x_copies[j].append((zz, remote(j, src, place(zz, j, xhi), device(2, 0, 0, 0))))

    def merge(j):
        for cp in b_copies[j]:
            cp.wait_recv()
        for r in range(ROUNDS):
            column = order_ref[r, blk] // 8

            def store(at, n, value):
                final[j][r, pl.ds(at, n), :] = value

            copy_rows(width(j), store, lambda at, n: b_recv[j][r, column, pl.ds(at, n), :])
        own = pltpu.make_async_copy(final[j], place(z, j, xhi), lsem.at[j, 1])
        own.start()
        locals_[j].append(own)
        if CHUNKS[j][2]:
            gather(j, final[j])
        else:
            x_copies[j].append((z, remote(j, final[j], place(z, j, xhi), device(2, 0, 0, 0))))

    def gather(j, src):
        up = remote(j, src, gathered(z, j), device(0, 0, 1, 0))
        down = remote(j, src, gathered(z, j), device(0, 0, -1, 0))
        spread(j, z, src)
        c_copies[j] = [up, down]

    def complete(j):
        x_copies[j][0][1].wait_recv()
        locals_[j][1].wait()
        gather(j, gathered(z, j))

    def forward(j):
        up, down = c_copies[j]
        up.wait_recv()
        part = place(below, j, xhi, 0)
        f_up = remote(j, part, part, device(0, 0, 1, 0))
        spread(j, below, gathered(below, j))
        down.wait_recv()
        part = place(above, j, xhi, 1)
        f_down = remote(j, part, part, device(0, 0, -1, 0))
        spread(j, above, gathered(above, j))
        c_copies[j] = [f_up, f_down]

    def forwarded(j):
        for cp in c_copies[j]:
            cp.wait_recv()
        spread(j, far, gathered(far, j))

    def crossed(j):
        for zz, cp in x_copies[j]:
            cp.wait_recv()
            part = place(zz, j, 1 - xhi)
            sides.append(remote(j, part, part, device(0, 0, 0, 1)))

    steps = {
        True: (pick_and_send, merge, forward, forwarded, crossed),
        False: (pick_and_send, merge, complete, forward, forwarded),
    }
    for j in range(AHEAD):
        start_a(j)
    for t in range(NCH + max(AGES)):
        for stage in (4, 3, 2, 1, 0):
            j = t - AGES[stage]
            if 0 <= j < NCH:
                steps[CHUNKS[j][2]][stage](j)
                if stage == 0 and j + AHEAD < NCH:
                    start_a(j + AHEAD)
    for cp in sides:
        cp.wait_recv()
    for j in range(NCH):
        if CHUNKS[j][2]:
            locals_[j][1].wait()
    for cp in everything:
        cp.wait_send()


def exchange(order, s):
    bf16 = jnp.bfloat16
    sizes = [(n, n // 2) for _, n, _ in CHUNKS]
    scratch = [pltpu.VMEM((8, n, CH), bf16) for n, _ in sizes]
    scratch += [pltpu.VMEM((ROUNDS, n, CH), bf16) for n, _ in sizes]
    scratch += [pltpu.VMEM((ROUNDS, 2, w, CH), bf16) for _, w in sizes]
    scratch += [pltpu.VMEM((ROUNDS, w, CH), bf16) for _, w in sizes]
    scratch += [
        pltpu.SemaphoreType.DMA((NCH, NSEM)),
        pltpu.SemaphoreType.DMA((NCH, NSEM)),
        pltpu.SemaphoreType.DMA((NCH, 2)),
    ]
    return pl.pallas_call(
        exchange_kernel,
        out_shape=jax.ShapeDtypeStruct((ROUNDS, 8, PIECE, CH), bf16),
        in_specs=[
            pl.BlockSpec(memory_space=pltpu.SMEM),
            pl.BlockSpec(memory_space=pl.ANY),
        ],
        out_specs=pl.BlockSpec(memory_space=pl.ANY),
        scratch_shapes=scratch,
        compiler_params=pltpu.CompilerParams(
            has_side_effects=True, vmem_limit_bytes=56 * 2**20
        ),
        name="exchange",
    )(order, s)


def cross_kernel(own_ref, other_ref, o_ref):
    own = own_ref[0].reshape(WIN // STEPW, 4, STEPW, CH)
    for b in range(2):
        p = own[:, 2 * b].reshape(WIN, CH)
        q = own[:, 2 * b + 1].reshape(WIN, CH)
        pt, qt = p.T, q.T
        left = jnp.concatenate(
            [jnp.concatenate([pt, qt], axis=1), jnp.concatenate([qt, -pt], axis=1)], axis=0
        )
        for r in range(ROUNDS):
            other = other_ref[r, 0].reshape(WIN // STEPW, 4, STEPW, CH)
            right = jnp.concatenate(
                [other[:, 2 * b].reshape(WIN, CH), other[:, 2 * b + 1].reshape(WIN, CH)], axis=0
            )
            out = jnp.dot(left, right, preferred_element_type=jnp.float32)
            out = (out * (1.0 / math.sqrt(WIN))).astype(jnp.bfloat16)
            o_ref[r, 0, b] = out[:CH]
            o_ref[r, 1, b] = out[CH:]


def cross(s, g):
    return pl.pallas_call(
        cross_kernel,
        grid=(8,),
        out_shape=jax.ShapeDtypeStruct((ROUNDS, 2, NB, CH, CH), jnp.bfloat16),
        in_specs=[
            pl.BlockSpec((1, PIECE, CH), lambda f: (f, 0, 0)),
            pl.BlockSpec((ROUNDS, 1, PIECE, CH), lambda f: (0, f, 0, 0)),
        ],
        out_specs=pl.BlockSpec((ROUNDS, 2, 2, CH, CH), lambda f: (0, 0, f, 0, 0)),
        compiler_params=pltpu.CompilerParams(vmem_limit_bytes=48 * 2**20),
        name="cross",
    )(s, g)


def body(record, owner_order):
    s = spectra(record)
    g = exchange(owner_order, s)
    return cross(s, g)


def solution(mesh):
    placed = (P(None, ("blk", "grp")), P())
    return jax.shard_map(
        body,
        mesh=mesh,
        in_specs=placed,
        out_specs=P(None, None, None, ("blk", "grp"), None),
        check_vma=False,
    )
```

time: 182 us -> 154 us (0.85)
  Pallas kernels: 178 us -> 150 us
    pallas_call x1, Pallas kernels: 149 us -> 121 us  [exchange(): pl.pallas_call(exchange_kernel, out_shape=jax.ShapeDtypeStruct((ROUNDS, 8...]
    pallas_call x1, Pallas kernels: 8.29 us -> 12.3 us  [spectra(): pl.pallas_call(spectra_kernel, grid=(steps,), out_shape=jax.ShapeDtypeStr...]
    pallas_call x1, Pallas kernels: 21 us -> 17.1 us  [cross(): pl.pallas_call(cross_kernel, grid=(8,), out_shape=jax.ShapeDtypeStruct((R...]
where the time goes in v2:
time: 154 us; the launch traced here: 153 us
  Pallas kernels  150 us (97%)
  local copies, waits for them, and re-layouts  2.98 us (2%)
    pallas_call x1, Pallas kernels, exchange(): pl.pallas_call(exchange_kernel, out_shape=jax.ShapeDtypeStruct((ROUNDS, 8...  121 us
    pallas_call x1, Pallas kernels, cross(): pl.pallas_call(cross_kernel, grid=(8,), out_shape=jax.ShapeDtypeStruct((R...  17.1 us
    pallas_call x1, Pallas kernels, spectra(): pl.pallas_call(spectra_kernel, grid=(steps,), out_shape=jax.ShapeDtypeStr...  12.3 us

profile of v2, /device:TPU:1, one launch (start us, length us, event | category | flops | bytes accessed | tf_op | source)
XLA Modules:
  0.0 153.2 jit_solution(14271436091806145344)
XLA Ops:
  0.0 0.0 copy-start.2
  0.0 1.0 copy-done.2
  1.0 12.3 %spectra.1 = bf16[8,16,4,16,256]{4,3,2,1,0:T(8,128)(2,1)S(1)} custom-call(bf16[256,576]{1,0:T(8,128)(2,1)S(1)} %copy-done.2, bf16[16448,256]{1,0:T(8,128)(2,1)} %tail_ref.1, bf16[16448,256]{1,0:T(8,128)(2,1)} %tail_ref.1), custom_call_target="tpu_custom_call" | custom-call | tf_op jit(solution)/shard_map/spectra/pallas_call | solution.py:68
  13.3 0.0 copy-start
  13.3 2.0 %copy-done = bf16[8,16,4,16,256]{4,3,2,1,0:T(8,128)(2,1)} copy-done((bf16[8,16,4,16,256]{4,3,2,1,0:T(8,128)(2,1)}, bf16[8,16,4,16,256]{4,3,2,1,0:T(8,128)(2,1)S(1)}, u32[]{:S(2)}) %copy-start) | copy-done | bytes 4194328
  15.3 0.0 copy-start.1
  15.3 120.8 %exchange.1.other_ref = bf16[4,8,1024,256]{3,2,1,0:T(8,128)(2,1)} custom-call(s32[4,8]{1,0:T(4,128)} %order_ref.1, bf16[8,1024,256]{2,1,0:T(8,128)(2,1)} %bitcast.1), custom_call_target="tpu_custom_call" | custom-call | tf_op jit(solution)/shard_map/exchange/pallas_call | solution.py:302
  136.1 0.0 copy-done.1
  136.1 17.1 %cross.1 = bf16[4,2,16,256,256]{4,3,2,1,0:T(8,128)(2,1)} custom-call(bf16[8,1024,256]{2,1,0:T(8,128)(2,1)S(1)} %bitcast.2, bf16[4,8,1024,256]{3,2,1,0:T(8,128)(2,1)} %exchange.1.other_ref), custom_call_target="tpu_custom_call" | custom-call | tf_op jit(solution)/shard_map/cross/pallas_call | solution.py:339
Async XLA Ops:
  0.0 1.0 copy-start.2
  13.3 2.0 %copy-start = (bf16[8,16,4,16,256]{4,3,2,1,0:T(8,128)(2,1)}, bf16[8,16,4,16,256]{4,3,2,1,0:T(8,128)(2,1)S(1)}, u32[]{:S(2)}) copy-start(bf16[8,16,4,16,256]{4,3,2,1,0:T(8,128)(2,1)S(1)} %spectra.1) | copy-start | bytes 12582916
  15.3 120.9 %copy-start.1 = (bf16[8,16,4,16,256]{4,3,2,1,0:T(8,128)(2,1)S(1)}, bf16[8,16,4,16,256]{4,3,2,1,0:T(8,128)(2,1)}, u32[]{:S(2)}) copy-start(bf16[8,16,4,16,256]{4,3,2,1,0:T(8,128)(2,1)} %copy-done) | copy-start | bytes 12582916

commit v3 on v2

--- a/solution.py
+++ b/solution.py
@@ -44,43 +44,6 @@
     return wide.reshape(2 * NB * GW, HOP * (GW + 1)).astype(jnp.bfloat16)
 
 
-def spectra_kernel(t_ref, main_ref, tail_ref, o_ref):
-    parts = []
-    for s in range(STEPW // GW):
-        lo = s * GW * HOP
-        if s < STEPW // GW - 1:
-            x = main_ref[lo : lo + (GW + 1) * HOP, :]
-        else:
-            x = jnp.concatenate([main_ref[lo : lo + GW * HOP, :], tail_ref[...]], axis=0)
-        raw = jnp.dot(t_ref[...], x, preferred_element_type=jnp.float32)
-        wide = x.astype(jnp.float32)
-        energy = jnp.sum((wide * wide).reshape(GW + 1, HOP, CH), axis=1)
-        inv = 1.0 / jnp.sqrt((energy[:GW] + energy[1:]) / NS + 1e-05)
-        parts.append(raw.reshape(2 * NB, GW, CH) * inv[None])
-        if s % 2 == 1:
-            both = jnp.concatenate(parts, axis=1).astype(jnp.bfloat16)
-            o_ref[:, 0, :, (s - 1) * GW : (s + 1) * GW, :] = both.reshape(8, 4, 2 * GW, CH)
-            parts = []
-
-
-def spectra(record):
-    steps = WIN // STEPW
-    out = pl.pallas_call(
-        spectra_kernel,
-        grid=(steps,),
-        out_shape=jax.ShapeDtypeStruct((8, steps, 4, STEPW, CH), jnp.bfloat16),
-        in_specs=[
-            pl.BlockSpec((2 * NB * GW, HOP * (GW + 1)), lambda g: (0, 0)),
-            pl.BlockSpec((STEPW * HOP, CH), lambda g: (g, 0)),
-            pl.BlockSpec((HOP, CH), lambda g: ((g + 1) * STEPW, 0)),
-        ],
-        out_specs=pl.BlockSpec((8, 1, 4, STEPW, CH), lambda g: (0, g, 0, 0, 0)),
-        compiler_params=pltpu.CompilerParams(vmem_limit_bytes=48 * 2**20),
-        name="spectra",
-    )(jnp.asarray(banded_table()), record, record)
-    return out.reshape(8, PIECE, CH)
-
-
 NSEM = 32
 WB_ROWS = 4 * STEPW
 CHUNKS = []
@@ -90,13 +53,15 @@
 NCH = len(CHUNKS)
 
 
-def exchange_kernel(order_ref, s_ref, g_ref, *scratch):
+def exchange_kernel(order_in, t_in, rec_ref, g_ref, own_ref, *scratch):
     it = iter(scratch)
+    order_ref, t_ref = next(it), next(it)
+    rec, s_ref = next(it), next(it)
     a_buf = [next(it) for _ in range(NCH)]
     b_send = [next(it) for _ in range(NCH)]
     b_recv = [next(it) for _ in range(NCH)]
     final = [next(it) for _ in range(NCH)]
-    ssem, rsem, lsem = next(it), next(it), next(it)
+    ssem, rsem, lsem, isem = next(it), next(it), next(it), next(it)
 
     blk = lax.axis_index("blk")
     grp = lax.axis_index("grp")
@@ -153,6 +118,52 @@
         if CHUNKS[j][2]:
             return place(zz, j, xhi)
         return g_ref.at[:, zz * 2 + core, pl.ds(CHUNKS[j][0], CHUNKS[j][1])]
+
+    small = [
+        pltpu.make_async_copy(t_in, t_ref, isem.at[2 * NCH]),
+        pltpu.make_async_copy(order_in, order_ref, isem.at[2 * NCH + 1]),
+    ]
+    small[0].start()
+    reads = []
+    for j in range(NCH):
+        lo = CHUNKS[j][0] // 4 * HOP + (HOP if j else 0)
+        hi = (CHUNKS[j][0] + CHUNKS[j][1]) // 4 * HOP + HOP
+        rows = pl.ds(lo, hi - lo)
+        reads.append(pltpu.make_async_copy(rec_ref.at[rows], rec.at[rows], isem.at[j]))
+        reads[j].start()
+
+    small[1].start()
+
+    def compute(j):
+        if j == 0:
+            small[0].wait()
+            small[1].wait()
+        reads[j].wait()
+        first = CHUNKS[j][0] // WB_ROWS
+
+        def run(i, carry):
+            block = first + i
+            parts = []
+            for half in range(STEPW // GW):
+                at = pl.multiple_of(block * (STEPW * HOP) + half * (GW * HOP), HOP)
+                x = rec[pl.ds(at, (GW + 1) * HOP), :]
+                raw = jnp.dot(t_ref[...], x, preferred_element_type=jnp.float32)
+                wide = x.astype(jnp.float32)
+                energy = jnp.sum((wide * wide).reshape(GW + 1, HOP, CH), axis=1)
+                inv = 1.0 / jnp.sqrt((energy[:GW] + energy[1:]) / NS + 1e-05)
+                parts.append(raw.reshape(2 * NB, GW, CH) * inv[None])
+            both = jnp.concatenate(parts, axis=1).astype(jnp.bfloat16)
+            rows = pl.ds(pl.multiple_of(block * WB_ROWS, WB_ROWS), WB_ROWS)
+            s_ref[:, rows, :] = both.reshape(8, WB_ROWS, CH)
+            return carry
+
+        lax.fori_loop(0, CHUNKS[j][1] // WB_ROWS, run, 0)
+        rows = pl.ds(CHUNKS[j][0], CHUNKS[j][1])
+        out = pltpu.make_async_copy(s_ref.at[:, rows], own_ref.at[:, rows], isem.at[NCH + j])
+        out.start()
+        outs.append(out)
+
+    outs = []
 
     a_copies = [[] for _ in range(NCH)]
     locals_ = [[] for _ in range(NCH)]
@@ -270,8 +281,11 @@
         False: (pick_and_send, merge, complete, forward, forwarded),
     }
     for j in range(AHEAD):
+        compute(j)
         start_a(j)
     for t in range(NCH + max(AGES)):
+        if t + AHEAD < NCH:
+            compute(t + AHEAD)
         for stage in (4, 3, 2, 1, 0):
             j = t - AGES[stage]
             if 0 <= j < NCH:
@@ -285,12 +299,17 @@
             locals_[j][1].wait()
     for cp in everything:
         cp.wait_send()
-
-
-def exchange(order, s):
+    for out in outs:
+        out.wait()
+
+
+def exchange(order, record):
     bf16 = jnp.bfloat16
     sizes = [(n, n // 2) for _, n, _ in CHUNKS]
-    scratch = [pltpu.VMEM((8, n, CH), bf16) for n, _ in sizes]
+    table = jnp.asarray(banded_table())
+    scratch = [pltpu.SMEM(order.shape, order.dtype), pltpu.VMEM(table.shape, bf16)]
+    scratch += [pltpu.VMEM(record.shape, bf16), pltpu.VMEM((8, PIECE, CH), bf16)]
+    scratch += [pltpu.VMEM((8, n, CH), bf16) for n, _ in sizes]
     scratch += [pltpu.VMEM((ROUNDS, n, CH), bf16) for n, _ in sizes]
     scratch += [pltpu.VMEM((ROUNDS, 2, w, CH), bf16) for _, w in sizes]
     scratch += [pltpu.VMEM((ROUNDS, w, CH), bf16) for _, w in sizes]
@@ -298,21 +317,26 @@
         pltpu.SemaphoreType.DMA((NCH, NSEM)),
         pltpu.SemaphoreType.DMA((NCH, NSEM)),
         pltpu.SemaphoreType.DMA((NCH, 2)),
+        pltpu.SemaphoreType.DMA((2 * NCH + 2,)),
     ]
     return pl.pallas_call(
         exchange_kernel,
-        out_shape=jax.ShapeDtypeStruct((ROUNDS, 8, PIECE, CH), bf16),
+        out_shape=(
+            jax.ShapeDtypeStruct((ROUNDS, 8, PIECE, CH), bf16),
+            jax.ShapeDtypeStruct((8, PIECE, CH), bf16),
+        ),
         in_specs=[
-            pl.BlockSpec(memory_space=pltpu.SMEM),
-            pl.BlockSpec(memory_space=pl.ANY),
+            pl.BlockSpec(memory_space=pltpu.HBM),
+            pl.BlockSpec(memory_space=pltpu.HBM),
+            pl.BlockSpec(memory_space=pltpu.HBM),
         ],
-        out_specs=pl.BlockSpec(memory_space=pl.ANY),
+        out_specs=(pl.BlockSpec(memory_space=pl.ANY), pl.BlockSpec(memory_space=pl.ANY)),
         scratch_shapes=scratch,
         compiler_params=pltpu.CompilerParams(
-            has_side_effects=True, vmem_limit_bytes=56 * 2**20
+            has_side_effects=True, vmem_limit_bytes=26 * 2**20
         ),
         name="exchange",
-    )(order, s)
+    )(*(pltpu.with_memory_space_constraint(v, pltpu.HBM) for v in (order, table, record)))
 
 
 def cross_kernel(own_ref, other_ref, o_ref):
@@ -345,14 +369,13 @@
             pl.BlockSpec((ROUNDS, 1, PIECE, CH), lambda f: (0, f, 0, 0)),
         ],
         out_specs=pl.BlockSpec((ROUNDS, 2, 2, CH, CH), lambda f: (0, 0, f, 0, 0)),
-        compiler_params=pltpu.CompilerParams(vmem_limit_bytes=48 * 2**20),
+        compiler_params=pltpu.CompilerParams(vmem_limit_bytes=12 * 2**20),
         name="cross",
     )(s, g)
 
 
 def body(record, owner_order):
-    s = spectra(record)
-    g = exchange(owner_order, s)
+    g, s = exchange(owner_order, record)
     return cross(s, g)
 
 

time: 154 us -> 134 us (0.87)
  Pallas kernels: 150 us -> 134 us
  local copies, waits for them, and re-layouts: 2.98 us -> 0 us
    pallas_call x2 -> x1, Pallas kernels: 133 us -> 121 us  [exchange(): pl.pallas_call(exchange_kernel, out_shape=(jax.ShapeDtypeStruct((ROUNDS,...]
    pallas_call x1, Pallas kernels: 17.1 us -> 12.8 us  [cross(): pl.pallas_call(cross_kernel, grid=(8,), out_shape=jax.ShapeDtypeStruct((R...]
    unnamed x6 -> x0, local copies, waits for them, and re-layouts: 2.98 us -> none
where the time goes in v3:
time: 134 us
  Pallas kernels  134 us (100%)
    pallas_call x1, Pallas kernels, exchange(): pl.pallas_call(exchange_kernel, out_shape=(jax.ShapeDtypeStruct((ROUNDS,...  121 us
    pallas_call x1, Pallas kernels, cross(): pl.pallas_call(cross_kernel, grid=(8,), out_shape=jax.ShapeDtypeStruct((R...  12.8 us

profile of v3, /device:TPU:1, one launch (start us, length us, event | category | flops | bytes accessed | tf_op | source)
XLA Modules:
  0.0 134.0 jit_solution(5836901421993546096)
XLA Ops:
  0.0 121.2 %exchange.1 = (bf16[4,8,1024,256]{3,2,1,0:T(8,128)(2,1)S(1)}, bf16[8,1024,256]{2,1,0:T(8,128)(2,1)S(1)}) custom-call(s32[4,8]{1,0:T(4,128)} %order_in.1, bf16[256,576]{1,0:T(8,128)(2,1)} %constant.2.clone.t_in, bf16[16448,256]{1,0:T(8,128)(2,1)} %rec_ref.1), custom_call_target="tpu_custom_call" | custom-call | tf_op jit(solution)/shard_map/exchange/pallas_call | solution.py:322
  121.2 12.8 %cross.1 = bf16[4,2,16,256,256]{4,3,2,1,0:T(8,128)(2,1)} custom-call(bf16[8,1024,256]{2,1,0:T(8,128)(2,1)S(1)} %get-tuple-element.7.own_ref, bf16[4,8,1024,256]{3,2,1,0:T(8,128)(2,1)S(1)} %get-tuple-element.8.other_ref), custom_call_target="tpu_custom_call" | custom-call | tf_op jit(solution)/shard_map/cross/pallas_call | solution.py:363

commit v4 on v3

--- a/solution.py
+++ b/solution.py
@@ -286,7 +286,7 @@
     for t in range(NCH + max(AGES)):
         if t + AHEAD < NCH:
             compute(t + AHEAD)
-        for stage in (4, 3, 2, 1, 0):
+        for stage in (0, 1, 2, 3, 4):
             j = t - AGES[stage]
             if 0 <= j < NCH:
                 steps[CHUNKS[j][2]][stage](j)
@@ -340,38 +340,38 @@
 
 
 def cross_kernel(own_ref, other_ref, o_ref):
-    own = own_ref[0].reshape(WIN // STEPW, 4, STEPW, CH)
-    for b in range(2):
-        p = own[:, 2 * b].reshape(WIN, CH)
-        q = own[:, 2 * b + 1].reshape(WIN, CH)
-        pt, qt = p.T, q.T
-        left = jnp.concatenate(
-            [jnp.concatenate([pt, qt], axis=1), jnp.concatenate([qt, -pt], axis=1)], axis=0
+    piece, parts = pl.program_id(0) // 2, pl.ds(pl.program_id(0) % 2 * 2, 2)
+    own = own_ref[piece, :, parts]
+    p, q = own[:, 0].reshape(WIN, CH), own[:, 1].reshape(WIN, CH)
+    pt, qt = p.T, q.T
+    left = jnp.concatenate(
+        [jnp.concatenate([pt, qt], axis=1), jnp.concatenate([qt, -pt], axis=1)], axis=0
+    )
+    for r in range(ROUNDS):
+        other = other_ref[r, piece, :, parts]
+        right = jnp.concatenate(
+            [other[:, 0].reshape(WIN, CH), other[:, 1].reshape(WIN, CH)], axis=0
         )
-        for r in range(ROUNDS):
-            other = other_ref[r, 0].reshape(WIN // STEPW, 4, STEPW, CH)
-            right = jnp.concatenate(
-                [other[:, 2 * b].reshape(WIN, CH), other[:, 2 * b + 1].reshape(WIN, CH)], axis=0
-            )
-            out = jnp.dot(left, right, preferred_element_type=jnp.float32)
-            out = (out * (1.0 / math.sqrt(WIN))).astype(jnp.bfloat16)
-            o_ref[r, 0, b] = out[:CH]
-            o_ref[r, 1, b] = out[CH:]
+        out = jnp.dot(left, right, preferred_element_type=jnp.float32)
+        out = (out * (1.0 / math.sqrt(WIN))).astype(jnp.bfloat16)
+        o_ref[r, 0, 0] = out[:CH]
+        o_ref[r, 1, 0] = out[CH:]
 
 
 def cross(s, g):
+    rows = (WIN // STEPW, 4, STEPW, CH)
     return pl.pallas_call(
         cross_kernel,
-        grid=(8,),
+        grid=(NB,),
         out_shape=jax.ShapeDtypeStruct((ROUNDS, 2, NB, CH, CH), jnp.bfloat16),
         in_specs=[
-            pl.BlockSpec((1, PIECE, CH), lambda f: (f, 0, 0)),
-            pl.BlockSpec((ROUNDS, 1, PIECE, CH), lambda f: (0, f, 0, 0)),
+            pl.BlockSpec(memory_space=pltpu.VMEM),
+            pl.BlockSpec(memory_space=pltpu.VMEM),
         ],
-        out_specs=pl.BlockSpec((ROUNDS, 2, 2, CH, CH), lambda f: (0, 0, f, 0, 0)),
+        out_specs=pl.BlockSpec((ROUNDS, 2, 1, CH, CH), lambda f: (0, 0, f, 0, 0)),
         compiler_params=pltpu.CompilerParams(vmem_limit_bytes=12 * 2**20),
         name="cross",
-    )(s, g)
+    )(s.reshape((8,) + rows), g.reshape((ROUNDS, 8) + rows))
 
 
 def body(record, owner_order):

time: 134 us -> 134 us (level)
    pallas_call x1, Pallas kernels: 12.8 us -> 14.4 us  [cross(): pl.pallas_call(cross_kernel, grid=(NB,), out_shape=jax.ShapeDtypeStruct((...]
where the time goes in v4:
time: 134 us
  Pallas kernels  134 us (100%)
    pallas_call x1, Pallas kernels, exchange(): pl.pallas_call(exchange_kernel, out_shape=(jax.ShapeDtypeStruct((ROUNDS,...  120 us
    pallas_call x1, Pallas kernels, cross(): pl.pallas_call(cross_kernel, grid=(NB,), out_shape=jax.ShapeDtypeStruct((...  14.4 us

profile of v4, /device:TPU:1, one launch (start us, length us, event | category | flops | bytes accessed | tf_op | source)
XLA Modules:
  0.0 134.4 jit_solution(16104459353987428131)
XLA Ops:
  0.0 120.0 %exchange.1 = (bf16[4,8,1024,256]{3,2,1,0:T(8,128)(2,1)S(1)}, bf16[8,1024,256]{2,1,0:T(8,128)(2,1)S(1)}) custom-call(s32[4,8]{1,0:T(4,128)} %order_in.1, bf16[256,576]{1,0:T(8,128)(2,1)} %constant.2.clone.t_in, bf16[16448,256]{1,0:T(8,128)(2,1)} %rec_ref.1), custom_call_target="tpu_custom_call" | custom-call | tf_op jit(solution)/shard_map/exchange/pallas_call | solution.py:322
  120.0 14.4 %cross.1 = bf16[4,2,16,256,256]{4,3,2,1,0:T(8,128)(2,1)} custom-call(bf16[8,16,4,16,256]{4,3,2,1,0:T(8,128)(2,1)S(1)} %bitcast.3, bf16[4,8,16,4,16,256]{5,4,3,2,1,0:T(8,128)(2,1)S(1)} %bitcast.2), custom_call_target="tpu_custom_call" | custom-call | tf_op jit(solution)/shard_map/cross/pallas_call | solution.py:363

commit v5 on v3

--- a/solution.py
+++ b/solution.py
@@ -286,7 +286,7 @@
     for t in range(NCH + max(AGES)):
         if t + AHEAD < NCH:
             compute(t + AHEAD)
-        for stage in (4, 3, 2, 1, 0):
+        for stage in (0, 1, 2, 3, 4):
             j = t - AGES[stage]
             if 0 <= j < NCH:
                 steps[CHUNKS[j][2]][stage](j)
@@ -340,7 +340,8 @@
 
 
 def cross_kernel(own_ref, other_ref, o_ref):
-    own = own_ref[0].reshape(WIN // STEPW, 4, STEPW, CH)
+    piece = pl.program_id(0)
+    own = own_ref[piece].reshape(WIN // STEPW, 4, STEPW, CH)
     for b in range(2):
         p = own[:, 2 * b].reshape(WIN, CH)
         q = own[:, 2 * b + 1].reshape(WIN, CH)
@@ -349,7 +350,7 @@
             [jnp.concatenate([pt, qt], axis=1), jnp.concatenate([qt, -pt], axis=1)], axis=0
         )
         for r in range(ROUNDS):
-            other = other_ref[r, 0].reshape(WIN // STEPW, 4, STEPW, CH)
+            other = other_ref[r, piece].reshape(WIN // STEPW, 4, STEPW, CH)
             right = jnp.concatenate(
                 [other[:, 2 * b].reshape(WIN, CH), other[:, 2 * b + 1].reshape(WIN, CH)], axis=0
             )
@@ -365,8 +366,8 @@
         grid=(8,),
         out_shape=jax.ShapeDtypeStruct((ROUNDS, 2, NB, CH, CH), jnp.bfloat16),
         in_specs=[
-            pl.BlockSpec((1, PIECE, CH), lambda f: (f, 0, 0)),
-            pl.BlockSpec((ROUNDS, 1, PIECE, CH), lambda f: (0, f, 0, 0)),
+            pl.BlockSpec(memory_space=pltpu.VMEM),
+            pl.BlockSpec(memory_space=pltpu.VMEM),
         ],
         out_specs=pl.BlockSpec((ROUNDS, 2, 2, CH, CH), lambda f: (0, 0, f, 0, 0)),
         compiler_params=pltpu.CompilerParams(vmem_limit_bytes=12 * 2**20),

time: 134 us -> 132 us (0.985)
  Pallas kernels: 134 us -> 132 us
where the time goes in v5:
time: 132 us
  Pallas kernels  132 us (100%)
    pallas_call x1, Pallas kernels, exchange(): pl.pallas_call(exchange_kernel, out_shape=(jax.ShapeDtypeStruct((ROUNDS,...  120 us
    pallas_call x1, Pallas kernels, cross(): pl.pallas_call(cross_kernel, grid=(8,), out_shape=jax.ShapeDtypeStruct((R...  11.7 us

profile of v5, /device:TPU:1, one launch (start us, length us, event | category | flops | bytes accessed | tf_op | source)
XLA Modules:
  0.0 131.7 jit_solution(16834056898334880998)
XLA Ops:
  0.0 120.0 %exchange.1 = (bf16[4,8,1024,256]{3,2,1,0:T(8,128)(2,1)S(1)}, bf16[8,1024,256]{2,1,0:T(8,128)(2,1)S(1)}) custom-call(s32[4,8]{1,0:T(4,128)} %order_in.1, bf16[256,576]{1,0:T(8,128)(2,1)} %constant.2.clone.t_in, bf16[16448,256]{1,0:T(8,128)(2,1)} %rec_ref.1), custom_call_target="tpu_custom_call" | custom-call | tf_op jit(solution)/shard_map/exchange/pallas_call | solution.py:322
  120.0 11.7 %cross.1 = bf16[4,2,16,256,256]{4,3,2,1,0:T(8,128)(2,1)} custom-call(bf16[8,1024,256]{2,1,0:T(8,128)(2,1)S(1)} %get-tuple-element.7.own_ref, bf16[4,8,1024,256]{3,2,1,0:T(8,128)(2,1)S(1)} %get-tuple-element.8.other_ref), custom_call_target="tpu_custom_call" | custom-call | tf_op jit(solution)/shard_map/cross/pallas_call | solution.py:364

commit v6 on v5

--- a/solution.py
+++ b/solution.py
@@ -341,11 +341,12 @@
 
 def cross_kernel(own_ref, other_ref, o_ref):
     piece = pl.program_id(0)
+    scale = jnp.bfloat16(1.0 / math.sqrt(WIN))
     own = own_ref[piece].reshape(WIN // STEPW, 4, STEPW, CH)
     for b in range(2):
         p = own[:, 2 * b].reshape(WIN, CH)
         q = own[:, 2 * b + 1].reshape(WIN, CH)
-        pt, qt = p.T, q.T
+        pt, qt = p.T * scale, q.T * scale
         left = jnp.concatenate(
             [jnp.concatenate([pt, qt], axis=1), jnp.concatenate([qt, -pt], axis=1)], axis=0
         )
@@ -355,7 +356,7 @@
                 [other[:, 2 * b].reshape(WIN, CH), other[:, 2 * b + 1].reshape(WIN, CH)], axis=0
             )
             out = jnp.dot(left, right, preferred_element_type=jnp.float32)
-            out = (out * (1.0 / math.sqrt(WIN))).astype(jnp.bfloat16)
+            out = out.astype(jnp.bfloat16)
             o_ref[r, 0, b] = out[:CH]
             o_ref[r, 1, b] = out[CH:]
 

time: 132 us -> 132 us (level)
  no operation moved by 1% of the time
where the time goes in v6:
time: 132 us
  Pallas kernels  132 us (100%)
    pallas_call x1, Pallas kernels, exchange(): pl.pallas_call(exchange_kernel, out_shape=(jax.ShapeDtypeStruct((ROUNDS,...  120 us
    pallas_call x1, Pallas kernels, cross(): pl.pallas_call(cross_kernel, grid=(8,), out_shape=jax.ShapeDtypeStruct((R...  11.7 us

profile of v6, /device:TPU:1, one launch (start us, length us, event | category | flops | bytes accessed | tf_op | source)
XLA Modules:
  0.0 131.7 jit_solution(10178386955430956181)
XLA Ops:
  0.0 120.0 %exchange.1 = (bf16[4,8,1024,256]{3,2,1,0:T(8,128)(2,1)S(1)}, bf16[8,1024,256]{2,1,0:T(8,128)(2,1)S(1)}) custom-call(s32[4,8]{1,0:T(4,128)} %order_in.1, bf16[256,576]{1,0:T(8,128)(2,1)} %constant.2.clone.t_in, bf16[16448,256]{1,0:T(8,128)(2,1)} %rec_ref.1), custom_call_target="tpu_custom_call" | custom-call | tf_op jit(solution)/shard_map/exchange/pallas_call | solution.py:322
  120.0 11.7 %cross.1 = bf16[4,2,16,256,256]{4,3,2,1,0:T(8,128)(2,1)} custom-call(bf16[8,1024,256]{2,1,0:T(8,128)(2,1)S(1)} %get-tuple-element.7.own_ref, bf16[4,8,1024,256]{3,2,1,0:T(8,128)(2,1)S(1)} %get-tuple-element.8.other_ref), custom_call_target="tpu_custom_call" | custom-call | tf_op jit(solution)/shard_map/cross/pallas_call | solution.py:365

commit v7 on v5

--- a/solution.py
+++ b/solution.py
@@ -187,7 +187,7 @@
         for cp in a_copies[j]:
             cp.wait_recv()
         w = width(j)
-        for r in range(ROUNDS):
+        for r in (3, 1, 2, 0):
             owner = order_ref[r, (blk + r) % 8] % 8
 
             if r == 0:

time: 132 us -> 132 us (level)
  no operation moved by 1% of the time
where the time goes in v7:
time: 132 us
  Pallas kernels  132 us (100%)
    pallas_call x1, Pallas kernels, exchange(): pl.pallas_call(exchange_kernel, out_shape=(jax.ShapeDtypeStruct((ROUNDS,...  120 us
    pallas_call x1, Pallas kernels, cross(): pl.pallas_call(cross_kernel, grid=(8,), out_shape=jax.ShapeDtypeStruct((R...  11.7 us

profile of v7, /device:TPU:1, one launch (start us, length us, event | category | flops | bytes accessed | tf_op | source)
XLA Modules:
  0.0 131.7 jit_solution(16337377993773773194)
XLA Ops:
  0.0 120.0 %exchange.1 = (bf16[4,8,1024,256]{3,2,1,0:T(8,128)(2,1)S(1)}, bf16[8,1024,256]{2,1,0:T(8,128)(2,1)S(1)}) custom-call(s32[4,8]{1,0:T(4,128)} %order_in.1, bf16[256,576]{1,0:T(8,128)(2,1)} %constant.2.clone.t_in, bf16[16448,256]{1,0:T(8,128)(2,1)} %rec_ref.1), custom_call_target="tpu_custom_call" | custom-call | tf_op jit(solution)/shard_map/exchange/pallas_call | solution.py:322
  120.0 11.7 %cross.1 = bf16[4,2,16,256,256]{4,3,2,1,0:T(8,128)(2,1)} custom-call(bf16[8,1024,256]{2,1,0:T(8,128)(2,1)S(1)} %get-tuple-element.7.own_ref, bf16[4,8,1024,256]{3,2,1,0:T(8,128)(2,1)S(1)} %get-tuple-element.8.other_ref), custom_call_target="tpu_custom_call" | custom-call | tf_op jit(solution)/shard_map/cross/pallas_call | solution.py:364
